TPU v7x, 512 devices: a whole 4x8x8 slice. The times are simulated.
512 devices in a mesh: section: 16 (over x, z_hi), tensor: 32 (over y, z_lo, core).
Axes of the slice: x: 4, y: 8, z: 8 (z_hi: 4, z_lo: 2; z = z_hi * 2 + z_lo), core: 2. Of those that a mesh axis runs over, the one named last changes fastest.
Arguments:
- x_in: bfloat16 [16, 512, 4096], P('section', 'tensor'), may hold values from -40 to 40
- grad_out: bfloat16 [16, 512, 4096], P('section', 'tensor'), may hold values from -50 to 50
- gain: float32 [16, 4096], P('section'), may hold values from 0.5 to 1.5
- w_val: bfloat16 [16, 4096, 4096], P('section', 'tensor'), may hold values from -0.09375 to 0.09375
- w_out: bfloat16 [16, 4096, 4096], P('section', 'tensor'), may hold values from -0.09375 to 0.09375
- filt: float32 [16, 3, 4096], P('section', None, 'tensor'), may hold values from -3 to 3
- tail: bfloat16 [16, 2, 4096], P('section', None, 'tensor'), may hold values from -6 to 6
- micro_index: int32 [16], P('section'), may hold values from 0 to 15
Outputs:
- grad_in: bfloat16 [16, 512, 4096], P('section', 'tensor')
- grad_w_val: bfloat16 [16, 4096, 4096], P('section', 'tensor')
- grad_w_out: bfloat16 [16, 4096, 4096], P('section', 'tensor')
- grad_filter: float32 [16, 3, 4096], P('section', None, 'tensor')
- grad_tail: float32 [16, 2, 4096], P('section', None, 'tensor')
- grad_gain: float32 [16, 4096], P('section')
All inputs are finite; a program needn't handle non-finite values.
Results may differ from a plain program's by a relative error of at most 0.023.
Values may be sent and summed in bfloat16 or wider, within the bound.
No kernel may reach another device: no remote copies, remote signals or barrier semaphores. Data moves between devices by JAX's collectives and lax.ppermute only.
A program may use at most 64 MiB of HBM per device.

v0:
```python
import jax
import jax.numpy as jnp
from jax import lax
from jax.sharding import PartitionSpec as P

TAPS = 3
EPSILON = 1e-06


def shifted(block, axis, distance):
    devices = range(lax.axis_size(axis))
    route = [((i - distance) % len(devices), i) for i in devices]
    return lax.ppermute(block, axis, route)


def contract_last(left, right):
    return lax.dot_general(
        left, right, (((1,), (1,)), ((), ())), preferred_element_type=jnp.float32
    )


def contract_first(left, right):
    return lax.dot_general(
        left, right, (((0,), (0,)), ((), ())), preferred_element_type=jnp.float32
    )


def on_device(x_in, grad_out, gain, w_val, w_out, filt, tail, micro_index):
    x_rows = x_in[0]
    cot_rows = grad_out[0]
    gain_row = gain[0]
    val_weight = w_val[0]
    out_weight = w_out[0]
    filters = filt[0]
    tail_rows = tail[0]
    has_tail = micro_index[0] > 0
    x_float = x_rows.astype(jnp.float32)
    inv_rms = lax.rsqrt(jnp.mean(x_float * x_float, axis=-1, keepdims=True) + EPSILON)
    normed = (x_float * inv_rms * gain_row).astype(jnp.bfloat16)
    normed_all = lax.all_gather(normed, "tensor", axis=0, tiled=True)
    seq_len = normed_all.shape[0]
    values = contract_last(normed_all, val_weight).astype(jnp.bfloat16)
    lead_rows = jnp.where(has_tail, tail_rows, jnp.zeros_like(tail_rows))
    extended = jnp.concatenate([lead_rows, values], axis=0).astype(jnp.float32)
    conv_out = filters[0] * extended[TAPS - 1 : TAPS - 1 + seq_len]
    for tap in range(1, TAPS):
        conv_out = conv_out + filters[tap] * extended[TAPS - 1 - tap : TAPS - 1 - tap + seq_len]
    gate_sig = jax.nn.sigmoid(conv_out)
    gated = (conv_out * gate_sig).astype(jnp.bfloat16)
    grad_gated = contract_last(lax.all_gather(cot_rows, "tensor", axis=0, tiled=True), out_weight)
    grad_wo = contract_first(gated, lax.all_gather(cot_rows, "tensor", axis=0, tiled=True))
    grad_conv = grad_gated * gate_sig * (1.0 + conv_out * (1.0 - gate_sig))
    grad_filter = jnp.stack(
        [
            jnp.sum(grad_conv * extended[TAPS - 1 - tap : TAPS - 1 - tap + seq_len], axis=0)
            for tap in range(TAPS)
        ]
    )
    padded = jnp.pad(grad_conv, ((TAPS - 1, TAPS - 1), (0, 0)))
    grad_ext = filters[0] * padded[0 : seq_len + TAPS - 1]
    for tap in range(1, TAPS):
        grad_ext = grad_ext + filters[tap] * padded[tap : tap + seq_len + TAPS - 1]
    grad_values = grad_ext[TAPS - 1 :].astype(jnp.bfloat16)
    grad_tail = jnp.where(has_tail, grad_ext[: TAPS - 1], jnp.zeros_like(grad_ext[: TAPS - 1]))
    grad_wv = contract_first(grad_values, normed_all)
    grad_normed = lax.psum_scatter(
        jnp.dot(grad_values, val_weight, preferred_element_type=jnp.float32).astype(jnp.bfloat16),
        "tensor",
        scatter_dimension=0,
        tiled=True,
    ).astype(jnp.float32)
    gain_term = jnp.sum(grad_normed * x_float * inv_rms, axis=0)
    grad_gain = lax.psum(gain_term, "tensor")
    scaled = gain_row * grad_normed
    grad_local = (
        cot_rows.astype(jnp.float32)
        + inv_rms * scaled
        - x_float * inv_rms**3 * jnp.mean(scaled * x_float, axis=-1, keepdims=True)
    )
    received = shifted(grad_local.astype(jnp.bfloat16), "section", -1)
    return (
        received[None],
        grad_wv.astype(jnp.bfloat16)[None],
        grad_wo.astype(jnp.bfloat16)[None],
        grad_filter[None],
        grad_tail[None],
        grad_gain[None],
    )


def solution(mesh):
    placed = (
        P("section", "tensor", None),
        P("section", "tensor", None),
        P("section", None),
        P("section", "tensor", None),
        P("section", "tensor", None),
        P("section", None, "tensor"),
        P("section", None, "tensor"),
        P("section"),
    )
    return jax.shard_map(
        on_device,
        mesh=mesh,
        in_specs=placed,
        out_specs=(
            P("section", "tensor", None),
            P("section", "tensor", None),
            P("section", "tensor", None),
            P("section", None, "tensor"),
            P("section", None, "tensor"),
            P("section", None),
        ),
        check_vma=False,
    )
```

profile of v0, /device:TPU:32, one launch (start us, length us, event | category | flops | bytes accessed | tf_op | source)
XLA Modules:
  0.0 413.5 jit_solution(13749967059140600081)
XLA Ops:
  7.2 0.0 copy-start
  7.2 0.0 copy-start.5
  7.2 0.0 all-gather.4.cloned.1.call-start
  7.2 1.2 fusion.18
  8.4 1.7 fusion.20
  10.1 0.0 all-gather.4.cloned.1.call-update
  10.1 0.0 all-gather.6.cloned.1.call-start
  10.2 0.7 all-gather.6.cloned.1.call-update
  10.9 0.0 reduce-scatter.2.cloned.1.call-start
  11.6 0.7 fusion.27
  12.2 0.7 slice_bitcast_fusion.2
  12.9 69.8 %all-gather.4.cloned.1.call-done = bf16[512,4096]{1,0:T(8,128)(2,1)} async-done(((bf16[16,4096]{1,0:T(8,128)(2,1)}), bf16[512,4096]{1,0:T(8,128)(2,1)}) %all-gather.4.cloned.1.call-update) | async-done | bytes 4194320 | tf_op jit(solution)/shard_map/all_gather | solution.py:40
  82.7 0.0 copy-done
  82.7 3.4 convolution_convert_fusion.3
  86.2 0.1 multiply_add_fusion.1
  86.3 67.6 %all-gather.6.cloned.1.call-done = bf16[1,512,4096]{2,1,0:T(8,128)(2,1)} async-done(((bf16[1,16,4096]{2,1,0:T(8,128)(2,1)}), bf16[1,512,4096]{2,1,0:T(8,128)(2,1)}) %all-gather.6.cloned.1.call-update) | async-done | bytes 4194320 | tf_op jit(solution)/shard_map/all_gather | solution.py:50
  153.9 0.0 copy-done.5
  153.9 3.5 multiply_reduce_fusion.2
  157.4 0.1 multiply_add_fusion
  157.5 3.2 convolution_convert_fusion
  160.7 0.0 reduce-scatter.2.cloned.1.call-update
  160.8 0.0 copy-start.1
  160.8 0.6 copy.14
  161.3 0.0 copy-start.2
  161.3 0.0 copy-start.4
  161.4 4.2 %fusion.1 = bf16[1,128,4096]{2,1,0:T(8,128)(2,1)} fusion(bf16[1,512,4096]{2,1,0:T(8,128)(2,1)} %all-gather.6.cloned.1.call-done, f32[512,128]{1,0:T(8,128)S(1)} %multiply_add_fusion.1), kind=kOutput, calls=%fused_computation.4 | convolution fusion | flops 537722880 | bytes 5505024 | tf_op jit(solution)/shard_map/dot_general | solution.py:23
  165.6 0.0 copy-done.1
  165.6 0.0 copy-start.3
  165.6 1.7 fusion
  167.3 120.2 %reduce-scatter.2.cloned.1.call-done = bf16[16,4096]{1,0:T(8,128)(2,1)} async-done(((bf16[512,4096]{1,0:T(8,128)(2,1)}), bf16[16,4096]{1,0:T(8,128)(2,1)}) %reduce-scatter.2.cloned.1.call-update) | async-done | bytes 131088 | tf_op jit(solution)/shard_map/reduce_scatter | solution.py:66
  287.6 0.0 copy-done.2
  287.6 0.0 copy-done.4
  287.6 1.2 fusion.24
  288.7 0.0 copy-done.3
  288.7 1.0 fusion.17
  289.8 7.5 %collective-permute-start = (bf16[16,4096]{1,0:T(8,128)(2,1)S(1)}, bf16[16,4096]{1,0:T(8,128)(2,1)S(1)}, u32[]{:S(2)}, u32[]{:S(2)}) collective-permute-start(bf16[16,4096]{1,0:T(8,128)(2,1)S(1)} %fusion.17), channel_id=1, source_target_pairs={{32,0},{64,32},{96,64},{128,96},{160,128},{192,160},{224,192},{256... | collective-permute-start | bytes 393224 | tf_op jit(solution)/shard_map/ppermute | solution.py:13
  297.3 0.6 fusion.26
  297.9 108.5 %psum.7 = f32[1,4096]{1,0:T(1,128)} all-reduce(f32[1,4096]{1,0:T(1,128)S(1)} %bitcast.60), channel_id=1, replica_groups=mesh['section'=16,'tensor'=32] {'tensor'}, use_global_device_ids=true, to_apply=%region_7.8 | all-reduce | flops 4096 | bytes 32768 | tf_op jit(solution)/shard_map/psum | solution.py:73
  406.3 0.0 collective-permute-done
  406.3 0.7 copy.17
  (4 shorter events, 0.1 us)
Async XLA Ops:
  7.2 75.6 %copy-start = (bf16[1,128,4096]{2,1,0:T(8,128)(2,1)S(1)}, bf16[1,128,4096]{2,1,0:T(8,128)(2,1)}, u32[]{:S(2)}) copy-start(bf16[1,128,4096]{2,1,0:T(8,128)(2,1)} %param.11) | copy-start | bytes 3145732
  7.2 146.8 %copy-start.5 = (bf16[1,128,4096]{2,1,0:T(8,128)(2,1)S(1)}, bf16[1,128,4096]{2,1,0:T(8,128)(2,1)}, u32[]{:S(2)}) copy-start(bf16[1,128,4096]{2,1,0:T(8,128)(2,1)} %param.12) | copy-start | bytes 3145732
  7.2 75.5 %all-gather.4.cloned.1.call-start = ((), (), s32[]{:S(2)}) async-start(), calls=%async_computation.1 | async-start | bytes 4325376 | tf_op jit(solution)/shard_map/all_gather | solution.py:40
  10.1 143.8 %all-gather.6.cloned.1.call-start = ((), (), s32[]{:S(2)}) async-start(), calls=%async_computation.3 | async-start | bytes 4325376 | tf_op jit(solution)/shard_map/all_gather | solution.py:50
  10.9 276.7 %reduce-scatter.2.cloned.1.call-start = ((), (), s32[]{:S(2)}) async-start(), calls=%async_computation.2 | async-start | bytes 4325376 | tf_op jit(solution)/shard_map/reduce_scatter | solution.py:66
  160.8 4.8 %copy-start.1 = (bf16[512,4096]{1,0:T(8,128)(2,1)S(1)}, bf16[512,4096]{1,0:T(8,128)(2,1)}, u32[]{:S(2)}) copy-start(bf16[512,4096]{1,0:T(8,128)(2,1)} %all-gather.4.cloned.1.call-done) | copy-start | bytes 12582916
  161.3 126.2 %copy-start.2 = (bf16[1,16,4096]{2,1,0:T(8,128)(2,1)S(1)}, bf16[1,16,4096]{2,1,0:T(8,128)(2,1)}, u32[]{:S(2)}) copy-start(bf16[1,16,4096]{2,1,0:T(8,128)(2,1)} %param.8) | copy-start | bytes 393220
  161.3 126.2 %copy-start.4 = (f32[1,4096]{1,0:T(1,128)S(1)}, f32[1,4096]{1,0:T(1,128)}, u32[]{:S(2)}) copy-start(f32[1,4096]{1,0:T(1,128)} %param.10) | copy-start | bytes 49156
  165.6 123.1 %copy-start.3 = (bf16[1,16,4096]{2,1,0:T(8,128)(2,1)S(1)}, bf16[1,16,4096]{2,1,0:T(8,128)(2,1)}, u32[]{:S(2)}) copy-start(bf16[1,16,4096]{2,1,0:T(8,128)(2,1)} %param.9) | copy-start | bytes 393220
  289.8 116.6 %collective-permute-start = (bf16[16,4096]{1,0:T(8,128)(2,1)S(1)}, bf16[16,4096]{1,0:T(8,128)(2,1)S(1)}, u32[]{:S(2)}, u32[]{:S(2)}) collective-permute-start(bf16[16,4096]{1,0:T(8,128)(2,1)S(1)} %fusion.17), channel_id=1, source_target_pairs={{32,0},{64,32},{96,64},{128,96},{160,128},{192,160},{224,192},{256... | collective-permute-start | bytes 393224 | tf_op jit(solution)/shard_map/ppermute | solution.py:13
Sparse Core Ops, SparseCore 0:
  10.7 71.9 all-gather.3
  84.9 69.0 all-gather.5
  160.9 126.6 reduce-scatter.1
where the time goes:
time: 414 us
  waiting for transfers between devices  258 us (62%)
  blocking collectives  108 us (26%)
  matrix products  16.1 us (4%)
  between operations  14.5 us (4%)
  starting transfers between devices  7.63 us (2%)
  other arithmetic  6.52 us (2%)
    reduce_scatter x1, waiting for transfers between devices, on_device(): lax.psum_scatter(jnp.dot(grad_values, val_weight, preferred_element_type=...  120 us
    psum x1, blocking collectives, on_device(): grad_gain = lax.psum(gain_term, 'tensor')  108 us
    all_gather x1, waiting for transfers between devices, on_device(): normed_all = lax.all_gather(normed, 'tensor', axis=0, tiled=True)  69.8 us
    all_gather x1, waiting for transfers between devices, on_device(): lax.all_gather(cot_rows, 'tensor', axis=0, tiled=True)  67.6 us
  transfers between devices with their start and end apart: 4, of which 3 were waited for; matrix products, arithmetic and copies ran while one was open for 3% of the time, Pallas kernels for 0%

commit v1 on v0

--- a/solution.py
+++ b/solution.py
@@ -5,6 +5,11 @@
 
 TAPS = 3
 EPSILON = 1e-06
+
+
+def add_all(array, axis):
+    parts = lax.all_gather(array, axis)
+    return jnp.sum(parts, axis=0)
 
 
 def shifted(block, axis, distance):
@@ -70,7 +75,7 @@
         tiled=True,
     ).astype(jnp.float32)
     gain_term = jnp.sum(grad_normed * x_float * inv_rms, axis=0)
-    grad_gain = lax.psum(gain_term, "tensor")
+    grad_gain = add_all(gain_term, "tensor")
     scaled = gain_row * grad_normed
     grad_local = (
         cot_rows.astype(jnp.float32)

time: 414 us -> 341 us (0.82)
  the two profiles are of different devices: /device:TPU:32 before, /device:TPU:1 now
where the time goes in v1:
time: 341 us
  waiting for transfers between devices  258 us (76%)
  blocking collectives  35.4 us (10%)
  matrix products  15.9 us (5%)
  between operations  14.5 us (4%)
  starting transfers between devices  7.58 us (2%)
  other arithmetic  7.17 us (2%)
    reduce_scatter x1, waiting for transfers between devices, on_device(): lax.psum_scatter(jnp.dot(grad_values, val_weight, preferred_element_type=...  117 us
    all_gather x1, waiting for transfers between devices, on_device(): normed_all = lax.all_gather(normed, 'tensor', axis=0, tiled=True)  73.1 us
    all_gather x1, waiting for transfers between devices, on_device(): lax.all_gather(cot_rows, 'tensor', axis=0, tiled=True)  67.6 us
    all_gather x1, blocking collectives, add_all(): parts = lax.all_gather(array, axis)  35.4 us
    ppermute x1, starting transfers between devices, shifted(): return lax.ppermute(block, axis, route)  7.46 us
    dot_general x2, matrix products, contract_last(): lax.dot_general(left, right, (((1,), (1,)), ((), ())), preferred_element_...  6.91 us
  transfers between devices with their start and end apart: 4, of which 3 were waited for; matrix products, arithmetic and copies ran while one was open for 4% of the time, Pallas kernels for 0%

profile of v1, /device:TPU:1, one launch (start us, length us, event | category | flops | bytes accessed | tf_op | source)
XLA Modules:
  0.0 341.0 jit_solution(7701724642571612917)
XLA Ops:
  7.2 0.0 copy-start
  7.2 0.0 copy-start.5
  7.2 0.0 all-gather.5.cloned.1.call-start
  7.2 1.2 fusion.18
  8.4 1.7 fusion.20
  10.1 0.0 all-gather.5.cloned.1.call-update
  10.1 0.0 all-gather.7.cloned.1.call-start
  10.2 0.7 all-gather.7.cloned.1.call-update
  10.9 0.0 reduce-scatter.2.cloned.1.call-start
  11.6 0.7 fusion.27
  12.2 0.7 slice_bitcast_fusion.2
  12.9 73.1 %all-gather.5.cloned.1.call-done = bf16[512,4096]{1,0:T(8,128)(2,1)} async-done(((bf16[16,4096]{1,0:T(8,128)(2,1)}), bf16[512,4096]{1,0:T(8,128)(2,1)}) %all-gather.5.cloned.1.call-update) | async-done | bytes 4194320 | tf_op jit(solution)/shard_map/all_gather | solution.py:45
  86.0 0.0 copy-done
  86.0 3.4 %convolution_convert_fusion.3 = bf16[512,128]{1,0:T(8,128)(2,1)S(1)} fusion(bf16[512,4096]{1,0:T(8,128)(2,1)} %all-gather.5.cloned.1.call-done, bf16[1,128,4096]{2,1,0:T(8,128)(2,1)S(1)} %copy-done), kind=kOutput, calls=%fused_computation.10 | convolution fusion | flops 536936448 | bytes 5373952 | tf_op jit(solution)/shard_map/dot_general | solution.py:22
  89.5 0.1 multiply_add_fusion.1
  89.6 67.6 %all-gather.7.cloned.1.call-done = bf16[1,512,4096]{2,1,0:T(8,128)(2,1)} async-done(((bf16[1,16,4096]{2,1,0:T(8,128)(2,1)}), bf16[1,512,4096]{2,1,0:T(8,128)(2,1)}) %all-gather.7.cloned.1.call-update) | async-done | bytes 4194320 | tf_op jit(solution)/shard_map/all_gather | solution.py:55
  157.2 0.0 copy-done.5
  157.2 3.5 %multiply_reduce_fusion.2 = (f32[128]{0:T(128)S(1)}, f32[128]{0:T(128)S(1)}, f32[128]{0:T(128)S(1)}, f32[512,128]{1,0:T(8,128)S(1)}) fusion(f32[514,128]{1,0:T(8,128)S(1)} %maximum_convert_fusion, f32[512,128]{1,0:T(8,128)S(1)} %multiply_add_fusion.1, bf16[1,128,4096]{2,1,0:T(8,128)(2,1)S(1)} %copy-done.5, ...), kind=kOutput, calls=%fused_computation.35 | convolution fusion | flops 537788032 | bytes 6555136 | tf_op jit(solution)/shard_map/dot_general | solution.py:22
  160.7 0.1 multiply_add_fusion
  160.8 3.2 convolution_convert_fusion
  164.0 0.0 reduce-scatter.2.cloned.1.call-update
  164.0 0.0 copy-start.1
  164.1 0.6 copy.16
  164.6 0.6 fusion.26
  165.2 0.0 copy-start.2
  165.2 0.0 copy-start.4
  165.2 4.0 %fusion.1 = bf16[1,128,4096]{2,1,0:T(8,128)(2,1)} fusion(bf16[1,512,4096]{2,1,0:T(8,128)(2,1)} %all-gather.7.cloned.1.call-done, f32[512,128]{1,0:T(8,128)S(1)} %multiply_add_fusion.1), kind=kOutput, calls=%fused_computation.4 | convolution fusion | flops 537722880 | bytes 5505024 | tf_op jit(solution)/shard_map/dot_general | solution.py:28
  169.2 0.0 copy-done.1
  169.2 0.0 copy-start.3
  169.2 1.7 fusion
  171.0 117.0 %reduce-scatter.2.cloned.1.call-done = bf16[16,4096]{1,0:T(8,128)(2,1)} async-done(((bf16[512,4096]{1,0:T(8,128)(2,1)}), bf16[16,4096]{1,0:T(8,128)(2,1)}) %reduce-scatter.2.cloned.1.call-update) | async-done | bytes 131088 | tf_op jit(solution)/shard_map/reduce_scatter | solution.py:71
  288.0 0.0 copy-done.2
  288.0 0.0 copy-done.4
  288.0 1.2 fusion.24
  289.1 0.0 copy-done.3
  289.1 1.0 fusion.17
  290.2 7.5 %collective-permute-start = (bf16[16,4096]{1,0:T(8,128)(2,1)S(1)}, bf16[16,4096]{1,0:T(8,128)(2,1)S(1)}, u32[]{:S(2)}, u32[]{:S(2)}) collective-permute-start(bf16[16,4096]{1,0:T(8,128)(2,1)S(1)} %fusion.17), channel_id=1, source_target_pairs={{32,0},{64,32},{96,64},{128,96},{160,128},{192,160},{224,192},{256... | collective-permute-start | bytes 393224 | tf_op jit(solution)/shard_map/ppermute | solution.py:18
  297.6 35.4 %all-gather.1 = f32[131072]{0:T(1024)S(1)} all-gather(f32[4096]{0:T(1024)S(1)} %get-tuple-element.27), channel_id=3, replica_groups=mesh['section'=16,'tensor'=32] {'tensor'}, dimensions={0}, use_global_device_ids=true | all-gather | bytes 540672 | tf_op jit(solution)/shard_map/all_gather | solution.py:11
  333.0 0.1 reshape.45
  333.1 0.7 reduce_sum.69
  333.8 0.0 collective-permute-done
  333.8 0.7 copy.19
  (4 shorter events, 0.1 us)
Async XLA Ops:
  7.2 78.9 %copy-start = (bf16[1,128,4096]{2,1,0:T(8,128)(2,1)S(1)}, bf16[1,128,4096]{2,1,0:T(8,128)(2,1)}, u32[]{:S(2)}) copy-start(bf16[1,128,4096]{2,1,0:T(8,128)(2,1)} %param.11) | copy-start | bytes 3145732
  7.2 150.1 %copy-start.5 = (bf16[1,128,4096]{2,1,0:T(8,128)(2,1)S(1)}, bf16[1,128,4096]{2,1,0:T(8,128)(2,1)}, u32[]{:S(2)}) copy-start(bf16[1,128,4096]{2,1,0:T(8,128)(2,1)} %param.12) | copy-start | bytes 3145732
  7.2 78.8 %all-gather.5.cloned.1.call-start = ((), (), s32[]{:S(2)}) async-start(), calls=%async_computation.1 | async-start | bytes 4325376 | tf_op jit(solution)/shard_map/all_gather | solution.py:45
  10.1 147.1 %all-gather.7.cloned.1.call-start = ((), (), s32[]{:S(2)}) async-start(), calls=%async_computation.3 | async-start | bytes 4325376 | tf_op jit(solution)/shard_map/all_gather | solution.py:55
  10.9 277.1 %reduce-scatter.2.cloned.1.call-start = ((), (), s32[]{:S(2)}) async-start(), calls=%async_computation.2 | async-start | bytes 4325376 | tf_op jit(solution)/shard_map/reduce_scatter | solution.py:71
  164.0 5.2 %copy-start.1 = (bf16[512,4096]{1,0:T(8,128)(2,1)S(1)}, bf16[512,4096]{1,0:T(8,128)(2,1)}, u32[]{:S(2)}) copy-start(bf16[512,4096]{1,0:T(8,128)(2,1)} %all-gather.5.cloned.1.call-done) | copy-start | bytes 12582916
  165.2 122.8 %copy-start.2 = (bf16[1,16,4096]{2,1,0:T(8,128)(2,1)S(1)}, bf16[1,16,4096]{2,1,0:T(8,128)(2,1)}, u32[]{:S(2)}) copy-start(bf16[1,16,4096]{2,1,0:T(8,128)(2,1)} %param.8) | copy-start | bytes 393220
  165.2 122.8 %copy-start.4 = (f32[1,4096]{1,0:T(1,128)S(1)}, f32[1,4096]{1,0:T(1,128)}, u32[]{:S(2)}) copy-start(f32[1,4096]{1,0:T(1,128)} %param.10) | copy-start | bytes 49156
  169.2 119.9 %copy-start.3 = (bf16[1,16,4096]{2,1,0:T(8,128)(2,1)S(1)}, bf16[1,16,4096]{2,1,0:T(8,128)(2,1)}, u32[]{:S(2)}) copy-start(bf16[1,16,4096]{2,1,0:T(8,128)(2,1)} %param.9) | copy-start | bytes 393220
  290.2 43.6 %collective-permute-start = (bf16[16,4096]{1,0:T(8,128)(2,1)S(1)}, bf16[16,4096]{1,0:T(8,128)(2,1)S(1)}, u32[]{:S(2)}, u32[]{:S(2)}) collective-permute-start(bf16[16,4096]{1,0:T(8,128)(2,1)S(1)} %fusion.17), channel_id=1, source_target_pairs={{32,0},{64,32},{96,64},{128,96},{160,128},{192,160},{224,192},{256... | collective-permute-start | bytes 393224 | tf_op jit(solution)/shard_map/ppermute | solution.py:18
Sparse Core Ops, SparseCore 0:
  10.7 75.2 all-gather.4
  88.2 69.0 all-gather.6
  164.2 123.7 reduce-scatter.1
